TPU v7x, 256 devices: a whole 4x4x8 slice. The times are simulated.
256 devices in a mesh: dp: 16 (over x, y), tensor: 16 (over z, core).
Axes of the slice: x: 4, y: 4, z: 8, core: 2. Of those that a mesh axis runs over, the one named last changes fastest.
Arguments:
- out_grad: bfloat16 [12288, 8192], P('dp', 'tensor'), may hold values from -6 to 6
- block_input: bfloat16 [12288, 8192], P('dp', 'tensor'), may hold values from -6 to 6
- gate_pre: bfloat16 [12288, 14336], P('dp', 'tensor'), may hold values from -8 to 8
- up_pre: bfloat16 [12288, 14336], P('dp', 'tensor'), may hold values from -6 to 6
- down_weight: bfloat16 [14336, 8192], P('tensor', 'dp'), may hold values from -0.046875 to 0.046875
- gate_in: bfloat16 [48, 16, 8192], P(None, None, 'tensor'), may hold values from -0.0625 to 0.0625
- gate_adapter_output_maps: bfloat16 [48, 16, 14336], P(None, None, 'tensor'), may hold values from -0.046875 to 0.046875
- up_in: bfloat16 [48, 16, 8192], P(None, None, 'tensor'), may hold values from -0.0625 to 0.0625
- up_adapter_output_maps: bfloat16 [48, 16, 14336], P(None, None, 'tensor'), may hold values from -0.046875 to 0.046875
- down_in: bfloat16 [48, 16, 14336], P(None, None, 'tensor'), may hold values from -0.046875 to 0.046875
- down_out: bfloat16 [48, 16, 8192], P(None, None, 'tensor'), may hold values from -0.0625 to 0.0625
- block_adapter: int32 [96], replicated, may hold values from 0 to 47, as said below
- owned_ids: int32 [48], replicated, may hold values from 0 to 47, as said below
Outputs:
- input_grad: bfloat16 [12288, 8192], P('dp', 'tensor')
- grad_gate_in: float32 [48, 16, 8192], P('dp', None, 'tensor')
- grad_gate_out: float32 [48, 16, 14336], P('dp', None, 'tensor')
- grad_up_in: float32 [48, 16, 8192], P('dp', None, 'tensor')
- grad_up_out: float32 [48, 16, 14336], P('dp', None, 'tensor')
- grad_down_in: float32 [48, 16, 14336], P('dp', None, 'tensor')
- grad_down_out: float32 [48, 16, 8192], P('dp', None, 'tensor')
Inputs may be any that keep to these rules, and one draw needn't show every extreme that they name: `block_adapter`: replica q (blocks q * 6 to q * 6 + 5) owns the adapters owned_ids[q * 3] to owned_ids[q * 3 + 2]. Among the 6 blocks of one replica, at most 1 names an adapter of any one owner; in every draw each replica has some owner that it names exactly once. `owned_ids`: each adapter appears once.
All inputs are finite; a program needn't handle non-finite values.
Results may differ from a plain program's by a relative error of at most 0.0058.
Values may be sent and summed in bfloat16 or wider, within the bound.
A program may use at most 128 MiB of HBM per device.

v0:
```python
import jax
import jax.numpy as jnp
from jax import lax
from jax.sharding import PartitionSpec as P

adapter_scale_factor = 2.0


def apply_projection(left, table):
    return jnp.einsum("nbd,nrd->nrb", left, table, preferred_element_type=jnp.float32)


def outer_product_sum(low, right):
    return jnp.einsum("nrb,nbw->nrw", low, right, preferred_element_type=jnp.float32)


def shards(
    out_grad,
    block_input,
    gate_pre,
    up_pre,
    down_weight,
    gate_in,
    gate_adapter_output_maps,
    up_in,
    up_adapter_output_maps,
    down_in,
    down_out,
    block_adapter,
    owned_ids,
):
    replicas = lax.axis_size("dp")
    replica = lax.axis_index("dp")
    tok_rows, width_part = out_grad.shape
    hidden_width_slice = gate_pre.shape[1]
    blocks_all = block_adapter.reshape(replicas, -1)
    block_count = blocks_all.shape[1]
    rows_per_block = tok_rows // block_count
    adapters = owned_ids.shape[0]
    owned = adapters // replicas
    capacity = (block_count + replicas - 1) // replicas
    my_ids = lax.dynamic_index_in_dim(blocks_all, replica, 0, keepdims=False)
    g_in = jnp.take(gate_in, my_ids, axis=0)
    gate_output_grad = jnp.take(gate_adapter_output_maps, my_ids, axis=0)
    u_in = jnp.take(up_in, my_ids, axis=0)
    up_output_grad = jnp.take(up_adapter_output_maps, my_ids, axis=0)
    input_dimension = jnp.take(down_in, my_ids, axis=0)
    d_out = jnp.take(down_out, my_ids, axis=0)
    output_grad_blocks = out_grad.reshape(block_count, rows_per_block, width_part)
    input_blocks = block_input.reshape(block_count, rows_per_block, width_part)
    gate_f = gate_pre.reshape(block_count, rows_per_block, hidden_width_slice).astype(jnp.float32)
    up_f = up_pre.reshape(block_count, rows_per_block, hidden_width_slice).astype(jnp.float32)
    hidden_activation = (jax.nn.silu(gate_f) * up_f).astype(jnp.bfloat16)
    partials = (
        apply_projection(input_blocks, g_in),
        apply_projection(input_blocks, u_in),
        apply_projection(hidden_activation, input_dimension),
        apply_projection(output_grad_blocks, d_out),
    )
    reduced = lax.psum((partials[0], partials[1], partials[2], partials[3]), "tensor")
    rank_gate_projection = reduced[0].astype(jnp.bfloat16)
    rank_up_projection = reduced[1].astype(jnp.bfloat16)
    rank_down_projection = reduced[2].astype(jnp.bfloat16)
    down_error_signal = reduced[3].astype(jnp.bfloat16)
    dy_full = lax.all_gather(out_grad, "tensor", axis=1, tiled=True)
    frozen_base_output = lax.dot_general(
        dy_full,
        lax.all_gather(down_weight, "dp", axis=1, tiled=True),
        (((1,), (1,)), ((), ())),
        preferred_element_type=jnp.float32,
    )
    hidden_gradient_rows = frozen_base_output.reshape(
        block_count, rows_per_block, hidden_width_slice
    ) + adapter_scale_factor * jnp.einsum(
        "elz,elp->ezp", down_error_signal, input_dimension, preferred_element_type=jnp.float32
    )
    sigmoid_gate = jax.nn.sigmoid(gate_f)
    gate_gradient_total = (
        hidden_gradient_rows * up_f * sigmoid_gate * (1.0 + gate_f * (1.0 - sigmoid_gate))
    ).astype(jnp.bfloat16)
    up_gradient_total = (hidden_gradient_rows * gate_f * sigmoid_gate).astype(jnp.bfloat16)
    returned = lax.psum(
        (
            adapter_scale_factor * apply_projection(gate_gradient_total, gate_output_grad),
            adapter_scale_factor * apply_projection(up_gradient_total, up_output_grad),
        ),
        "tensor",
    )
    gate_backward = returned[0].astype(jnp.bfloat16)
    up_backward = returned[1].astype(jnp.bfloat16)
    input_grad = jnp.einsum(
        "nrb,nrd->nbd", gate_backward, g_in, preferred_element_type=jnp.float32
    ) + jnp.einsum("nrb,nrd->nbd", up_backward, u_in, preferred_element_type=jnp.float32)
    input_grad = input_grad.astype(jnp.bfloat16).reshape(tok_rows, width_part)
    packet = jnp.concatenate(
        [
            outer_product_sum(gate_backward, input_blocks),
            adapter_scale_factor * outer_product_sum(rank_gate_projection, gate_gradient_total),
            outer_product_sum(up_backward, input_blocks),
            adapter_scale_factor * outer_product_sum(rank_up_projection, up_gradient_total),
            adapter_scale_factor * outer_product_sum(down_error_signal, hidden_activation),
            adapter_scale_factor * outer_product_sum(rank_down_projection, output_grad_blocks),
        ],
        axis=2,
    )
    order_index = jnp.arange(adapters, dtype=jnp.int32)
    rank_of = jnp.sum(
        jnp.where(owned_ids[None, :] == order_index[:, None], order_index[None, :], 0), axis=1
    )
    position = jnp.take(rank_of, blocks_all)
    target_all = position // owned
    local_all = position % owned
    block_index = jnp.arange(block_count, dtype=jnp.int32)
    earlier = block_index[:, None] > block_index[None, :]
    same_target = target_all[:, :, None] == target_all[:, None, :]
    slot_all = jnp.sum(jnp.logical_and(same_target, earlier[None, :, :]).astype(jnp.int32), axis=2)
    my_target = lax.dynamic_index_in_dim(target_all, replica, 0, keepdims=False)
    my_slot = lax.dynamic_index_in_dim(slot_all, replica, 0, keepdims=False)
    replica_index = jnp.arange(replicas, dtype=jnp.int32)
    slot_index = jnp.arange(capacity, dtype=jnp.int32)
    owned_index = jnp.arange(owned, dtype=jnp.int32)
    send_table = jnp.logical_and(
        my_target[None, None, :] == replica_index[:, None, None],
        my_slot[None, None, :] == slot_index[None, :, None],
    ).astype(jnp.float32)
    outgoing = jnp.einsum("qcn,nrw->qcrw", send_table, packet, precision=lax.Precision.HIGHEST)
    mine = (target_all == replica)[:, None, :, None]
    slot_match = slot_all[:, None, :, None] == slot_index[None, :, None, None]
    local_match = local_all[:, None, :, None] == owned_index[None, None, None, :]
    receive_table = jnp.sum(
        jnp.logical_and(jnp.logical_and(mine, slot_match), local_match).astype(jnp.float32), axis=2
    )
    owned_grads = jnp.einsum(
        "qco,qckw->okw",
        receive_table,
        lax.all_to_all(
            outgoing.astype(jnp.bfloat16), "dp", split_axis=0, concat_axis=0, tiled=True
        ).astype(outgoing.dtype),
        precision=lax.Precision.HIGHEST,
    )
    second = width_part + hidden_width_slice
    third = second + width_part
    fourth = third + hidden_width_slice
    fifth = fourth + hidden_width_slice
    return (
        input_grad,
        owned_grads[:, :, :width_part],
        owned_grads[:, :, width_part:second],
        owned_grads[:, :, second:third],
        owned_grads[:, :, third:fourth],
        owned_grads[:, :, fourth:fifth],
        owned_grads[:, :, fifth:],
    )


def solution(mesh):
    in_specs = (
        P("dp", "tensor"),
        P("dp", "tensor"),
        P("dp", "tensor"),
        P("dp", "tensor"),
        P("tensor", "dp"),
        P(None, None, "tensor"),
        P(None, None, "tensor"),
        P(None, None, "tensor"),
        P(None, None, "tensor"),
        P(None, None, "tensor"),
        P(None, None, "tensor"),
        P(),
        P(),
    )
    out_specs = (
        P("dp", "tensor"),
        P("dp", None, "tensor"),
        P("dp", None, "tensor"),
        P("dp", None, "tensor"),
        P("dp", None, "tensor"),
        P("dp", None, "tensor"),
        P("dp", None, "tensor"),
    )
    return jax.shard_map(shards, mesh=mesh, in_specs=in_specs, out_specs=out_specs, check_vma=False)
```

profile of v0, /device:TPU:112, one launch (start us, length us, event | category | flops | bytes accessed | tf_op | source)
XLA Modules:
  0.0 331.0 jit_solution(10830039742640613778)
XLA Ops:
  7.2 0.7 all-gather.3.cloned.1.call-update
  8.0 0.7 all-gather.5.cloned.1.call-update
  9.2 1.2 gather_fusion
  10.7 0.7 dynamic-slice_reduce_fusion
  11.4 1.7 gather_fusion.6
  13.4 1.7 gather_fusion.4
  15.1 1.0 fusion.30
  16.1 2.3 gather_fusion.2
  18.5 1.2 gather_fusion.3
  19.7 1.9 gather_fusion.5
  21.6 1.9 gather_fusion.1
  23.6 0.7 fusion.47
  24.4 1.2 fusion.23
  25.6 50.8 %psum.42 = bf16[6,16,128]{2,1,0:T(8,128)(2,1)S(1)} all-reduce(f32[6,16,128]{2,1,0:T(8,128)S(1)} %fusion.23), channel_id=1, replica_groups=mesh['dp'=16,'tensor'=16] {'tensor'}, use_global_device_ids=true, to_apply=%region_0.0 | all-reduce | flops 12288 | bytes 73728 | tf_op jit(solution)/shard_map/psum | solution.py:60
  76.4 10.7 %all-gather.3.cloned.1.call-done = bf16[768,8192]{1,0:T(8,128)(2,1)} async-done(((bf16[768,512]{1,0:T(8,128)(2,1)}), bf16[768,8192]{1,0:T(8,128)(2,1)}) %all-gather.3.cloned.1.call-update) | async-done | bytes 12582928 | tf_op jit(solution)/shard_map/all_gather | solution.py:65
  87.2 114.3 %all-gather.5.cloned.1.call-done = bf16[896,8192]{1,0:T(8,128)(2,1)} async-done(((bf16[896,512]{1,0:T(8,128)(2,1)}), bf16[896,8192]{1,0:T(8,128)(2,1)}) %all-gather.5.cloned.1.call-update) | async-done | bytes 14680080 | tf_op jit(solution)/shard_map/all_gather | solution.py:68
  201.5 17.9 %fusion.63 = f32[768,896]{1,0:T(8,128)S(1)} fusion(bf16[768,8192]{1,0:T(8,128)(2,1)} %all-gather.3.cloned.1.call-done, bf16[896,8192]{1,0:T(8,128)(2,1)} %all-gather.5.cloned.1.call-done), kind=kOutput, calls=%fused_computation.110 | convolution fusion | flops 11274289152 | bytes 30015488 | tf_op jit(solution)/shard_map/dot_general | solution.py:66
  219.5 2.2 fusion.10
  221.7 1.1 copy-done.3
  224.5 47.3 %all-reduce.2 = (bf16[6,16,128]{2,1,0:T(8,128)(2,1)S(1)}, bf16[6,16,128]{2,1,0:T(8,128)(2,1)S(1)}, bf16[6,16,128]{2,1,0:T(8,128)(2,1)S(1)}, bf16[6,16,128]{2,1,0:T(8,128)(2,1)S(1)}, bf16[6,16,128]{2,1,0:T(8,128)(2,1)S(1)}) all-reduce(f32[6,16,128]{2,1,0:T(8,128)S(1)} %convolution_multiply_fusion.5,, ...), channel_id=1, replica_groups=mesh['dp'=16,'tensor'=16] {'tensor'}, use_global_device_ids=true, to_apply=%region_1.4 | all-reduce | flops 61440 | bytes 368640 | tf_op jit(solution)/shard_map/psum | solution.py:82
  272.4 1.7 fusion.17
  274.7 0.8 copy-done.4
  276.1 2.6 fusion
  278.8 1.7 copy.59
  280.5 6.9 %all-to-all-start = ((bf16[16,1,16,4224]{3,2,1,0:T(8,128)(2,1)}), bf16[16,1,16,4224]{3,2,1,0:T(8,128)(2,1)S(1)}, u32[]{:S(2)}, u32[]{:S(2)}) async-start(bf16[16,1,16,4224]{3,2,1,0:T(8,128)(2,1)} %copy.59), calls=%async_computation | async-start | bytes 4325376 | tf_op jit(solution)/shard_map/all_to_all | solution.py:136
  287.5 1.3 fusion.31
  288.8 1.3 add_convert_fusion
  290.1 28.6 %all-to-all-done = bf16[16,1,16,4224]{3,2,1,0:T(8,128)(2,1)S(1)} async-done(((bf16[16,1,16,4224]{3,2,1,0:T(8,128)(2,1)}), bf16[16,1,16,4224]{3,2,1,0:T(8,128)(2,1)S(1)}, u32[]{:S(2)}, u32[]{:S(2)}) %all-to-all-start) | async-done | bytes 2162720 | tf_op jit(solution)/shard_map/all_to_all | solution.py:136
  318.7 1.1 fusion.11
  320.1 0.7 copy.65
  322.8 0.7 copy.64
  323.4 0.7 copy.62
  (77 shorter events, 7.0 us)
Async XLA Ops:
  7.2 11.3 %copy-start = (bf16[48,16,896]{2,1,0:T(8,128)(2,1)S(1)}, bf16[48,16,896]{2,1,0:T(8,128)(2,1)}, u32[]{:S(2)}) copy-start(bf16[48,16,896]{2,1,0:T(8,128)(2,1)} %param.26) | copy-start | bytes 4128772
  7.2 1.5 copy-start.20
  7.2 1.9 copy-start.23
  7.2 80.0 %all-gather.3.cloned.1.call-start = ((), (), s32[]{:S(2)}) async-start(), calls=%async_computation.1 | async-start | bytes 13369344 | tf_op jit(solution)/shard_map/all_gather | solution.py:65
  7.9 193.5 %all-gather.5.cloned.1.call-start = ((), (), s32[]{:S(2)}) async-start(), calls=%async_computation.2 | async-start | bytes 15597568 | tf_op jit(solution)/shard_map/all_gather | solution.py:68
  9.2 3.8 %copy-start.1 = (bf16[768,512]{1,0:T(8,128)(2,1)S(1)}, bf16[768,512]{1,0:T(8,128)(2,1)}, u32[]{:S(2)}) copy-start(bf16[768,512]{1,0:T(8,128)(2,1)} %param.18) | copy-start | bytes 2359300
  13.0 10.5 %copy-start.8 = (bf16[6,16,512]{2,1,0:T(8,128)(2,1)}, bf16[6,16,512]{2,1,0:T(8,128)(2,1)S(1)}, u32[]{:S(2)}) copy-start(bf16[6,16,512]{2,1,0:T(8,128)(2,1)S(1)} %gather_fusion.6) | copy-start | bytes 294916
  13.1 11.3 %copy-start.2 = (bf16[768,512]{1,0:T(8,128)(2,1)S(1)}, bf16[768,512]{1,0:T(8,128)(2,1)}, u32[]{:S(2)}) copy-start(bf16[768,512]{1,0:T(8,128)(2,1)} %param.17) | copy-start | bytes 2359300
  15.1 204.3 %copy-start.10 = (bf16[6,16,512]{2,1,0:T(8,128)(2,1)}, bf16[6,16,512]{2,1,0:T(8,128)(2,1)S(1)}, u32[]{:S(2)}) copy-start(bf16[6,16,512]{2,1,0:T(8,128)(2,1)S(1)} %gather_fusion.4) | copy-start | bytes 294916
  76.4 143.0 %copy-start.15 = (bf16[6,16,128]{2,1,0:T(8,128)(2,1)}, bf16[6,16,128]{2,1,0:T(8,128)(2,1)S(1)}, u32[]{:S(2)}) copy-start(bf16[6,16,128]{2,1,0:T(8,128)(2,1)S(1)} %psum.42) | copy-start | bytes 73732
  201.5 18.0 %copy-start.11 = (bf16[6,16,896]{2,1,0:T(8,128)(2,1)S(1)}, bf16[6,16,896]{2,1,0:T(8,128)(2,1)}, u32[]{:S(2)}) copy-start(bf16[6,16,896]{2,1,0:T(8,128)(2,1)} %gather_fusion.3) | copy-start | bytes 516100
  201.5 18.0 %copy-start.21 = (bf16[768,896]{1,0:T(8,128)(2,1)S(1)}, bf16[768,896]{1,0:T(8,128)(2,1)}, u32[]{:S(2)}) copy-start(bf16[768,896]{1,0:T(8,128)(2,1)} %param.19) | copy-start | bytes 4128772
  201.5 18.0 %copy-start.22 = (bf16[768,896]{1,0:T(8,128)(2,1)S(1)}, bf16[768,896]{1,0:T(8,128)(2,1)}, u32[]{:S(2)}) copy-start(bf16[768,896]{1,0:T(8,128)(2,1)} %param.20) | copy-start | bytes 4128772
  221.7 1.1 copy-start.3
  221.7 1.6 copy-start.5
  221.7 2.2 copy-start.7
  223.3 1.1 copy-start.12
  271.8 0.6 copy-start.17
  271.8 2.5 copy-start.13
  272.0 2.3 copy-start.6
  274.1 1.3 copy-start.4
  274.1 1.4 copy-start.16
  275.5 0.7 copy-start.18
  275.5 0.7 copy-start.19
  280.5 38.3 %all-to-all-start = ((bf16[16,1,16,4224]{3,2,1,0:T(8,128)(2,1)}), bf16[16,1,16,4224]{3,2,1,0:T(8,128)(2,1)S(1)}, u32[]{:S(2)}, u32[]{:S(2)}) async-start(bf16[16,1,16,4224]{3,2,1,0:T(8,128)(2,1)} %copy.59), calls=%async_computation | async-start | bytes 4325376 | tf_op jit(solution)/shard_map/all_to_all | solution.py:136
  287.4 1.4 copy-start.9
  287.4 1.4 copy-start.14
Sparse Core Ops, SparseCore 0:
  9.9 77.2 all-gather.2
  89.6 111.8 all-gather.4
where the time goes:
time: 331 us
  waiting for transfers between devices  155 us (47%)
  blocking collectives  98.1 us (30%)
  matrix products  33.8 us (10%)
  local copies, waits for them, and re-layouts  21.6 us (7%)
  between operations  14.4 us (4%)
  starting transfers between devices  7.01 us (2%)
    all_gather x1, waiting for transfers between devices, shards(): lax.all_gather(down_weight, 'dp', axis=1, tiled=True)  114 us
    psum x1, blocking collectives, shards(): lax.psum((partials[0], partials[1], partials[2], partials[3]), 'tensor')  50.8 us
    psum x1, blocking collectives, shards(): lax.psum((adapter_scale_factor * apply_projection(gate_gradient_total, ga...  47.3 us
    all_to_all x1, waiting for transfers between devices, shards(): lax.all_to_all(outgoing.astype(jnp.bfloat16), 'dp', split_axis=0, concat_...  28.6 us
    dot_general x1, matrix products, shards(): lax.dot_general(dy_full, lax.all_gather(down_weight, 'dp', axis=1, tiled=...  17.9 us
    all_gather x1, waiting for transfers between devices, shards(): dy_full = lax.all_gather(out_grad, 'tensor', axis=1, tiled=True)  10.7 us
    all_to_all x1, starting transfers between devices, shards(): lax.all_to_all(outgoing.astype(jnp.bfloat16), 'dp', split_axis=0, concat_...  6.93 us
  transfers between devices with their start and end apart: 3, of which 3 were waited for; matrix products, arithmetic and copies ran while one was open for 6% of the time, Pallas kernels for 0%

commit v1 on v0

--- a/solution.py
+++ b/solution.py
@@ -65,7 +65,9 @@
     dy_full = lax.all_gather(out_grad, "tensor", axis=1, tiled=True)
     frozen_base_output = lax.dot_general(
         dy_full,
-        lax.all_gather(down_weight, "dp", axis=1, tiled=True),
+        jnp.concatenate(
+            lax.all_to_all(jnp.stack([down_weight] * lax.axis_size("dp")), "dp", 0, 0), axis=1
+        ),
         (((1,), (1,)), ((), ())),
         preferred_element_type=jnp.float32,
     )

time: 331 us -> 457 us (1.38)
  local copies, waits for them, and re-layouts: 21.6 us -> 66.3 us
  waiting for transfers between devices: 155 us -> 198 us
  starting transfers between devices: 7.01 us -> 36.8 us
  matrix products: 33.8 us -> 41.5 us
    all_to_all x0 -> x1, waiting for transfers between devices: none -> 168 us  [shards(): lax.all_to_all(jnp.stack([down_weight] * lax.axis_size('dp')), 'dp', 0, 0)]
    all_gather x1 -> x0, waiting for transfers between devices: 114 us -> none  [shards(): lax.all_gather(down_weight, 'dp', axis=1, tiled=True)]
    reshape x0 -> x2, local copies, waits for them, and re-layouts: none -> 39 us  [shards(): jnp.concatenate(lax.all_to_all(jnp.stack([down_weight] * lax.axis_size('d...]
    all_to_all x1, starting transfers between devices: 6.93 us -> 29.3 us  [shards(): lax.all_to_all(outgoing.astype(jnp.bfloat16), 'dp', split_axis=0, concat_...]
    all_gather x1, waiting for transfers between devices: 10.7 us -> 0.01 us  [shards(): dy_full = lax.all_gather(out_grad, 'tensor', axis=1, tiled=True)]
    another operation x0 -> x1, local copies, waits for them, and re-layouts: none -> 7.74 us  [shards(): jnp.stack([down_weight] * lax.axis_size('dp'))]
    all_to_all x0 -> x1, starting transfers between devices: none -> 7.41 us  [shards(): lax.all_to_all(jnp.stack([down_weight] * lax.axis_size('dp')), 'dp', 0, 0)]
    dot_general x1, matrix products: 17.9 us -> 24.1 us  [shards(): lax.dot_general(dy_full, jnp.concatenate(lax.all_to_all(jnp.stack([down_w...]
  transfers between devices with their start and end apart: 3 -> 3, of which waited for: 3 -> 2; matrix products, arithmetic and copies ran while one was open for 6% -> 15% of each run, Pallas kernels for 0% -> 0%
where the time goes in v1:
time: 457 us; the launch traced here: 456 us
  waiting for transfers between devices  198 us (43%)
  blocking collectives  98 us (21%)
  local copies, waits for them, and re-layouts  66.3 us (15%)
  matrix products  41.5 us (9%)
  starting transfers between devices  36.8 us (8%)
  between operations  14.4 us (3%)
    all_to_all x1, waiting for transfers between devices, shards(): lax.all_to_all(jnp.stack([down_weight] * lax.axis_size('dp')), 'dp', 0, 0)  168 us
    psum x1, blocking collectives, shards(): lax.psum((partials[0], partials[1], partials[2], partials[3]), 'tensor')  50.1 us
    psum x1, blocking collectives, shards(): lax.psum((adapter_scale_factor * apply_projection(gate_gradient_total, ga...  47.8 us
    reshape x2, local copies, waits for them, and re-layouts, shards(): jnp.concatenate(lax.all_to_all(jnp.stack([down_weight] * lax.axis_size('d...  39 us
    all_to_all x1, starting transfers between devices, shards(): lax.all_to_all(outgoing.astype(jnp.bfloat16), 'dp', split_axis=0, concat_...  29.3 us
    all_to_all x1, waiting for transfers between devices, shards(): lax.all_to_all(outgoing.astype(jnp.bfloat16), 'dp', split_axis=0, concat_...  29.1 us
    dot_general x1, matrix products, shards(): lax.dot_general(dy_full, jnp.concatenate(lax.all_to_all(jnp.stack([down_w...  24.1 us
  transfers between devices with their start and end apart: 3, of which 2 were waited for; matrix products, arithmetic and copies ran while one was open for 15% of the time, Pallas kernels for 0%

profile of v1, /device:TPU:112, one launch (start us, length us, event | category | flops | bytes accessed | tf_op | source)
XLA Modules:
  0.0 455.7 jit_solution(3300854580797842740)
XLA Ops:
  7.2 0.7 all-gather.2.cloned.1.call-update
  7.9 7.7 %stack.2 = bf16[16,896,512]{2,1,0:T(8,128)(2,1)} broadcast(bf16[896,512]{1,0:T(8,128)(2,1)} %param.21), dimensions={1,2} | broadcast | bytes 15597568 | tf_op jit(solution)/shard_map/stack | solution.py:69
  15.7 7.4 %all-to-all-start = ((bf16[16,896,512]{2,1,0:T(8,128)(2,1)}), bf16[16,896,512]{2,1,0:T(8,128)(2,1)}, u32[]{:S(2)}, u32[]{:S(2)}) async-start(bf16[16,896,512]{2,1,0:T(8,128)(2,1)} %stack.2), calls=%async_computation | async-start | bytes 29360128 | tf_op jit(solution)/shard_map/all_to_all | solution.py:69
  23.4 1.7 gather_fusion.2
  25.7 2.0 gather_fusion.5
  27.7 1.9 gather_fusion.1
  29.6 1.7 gather_fusion.4
  31.9 1.0 fusion.31
  32.9 1.8 gather_fusion.6
  34.7 1.0 fusion.33
  35.9 1.2 gather_fusion
  37.4 0.7 dynamic-slice_reduce_fusion
  38.2 0.8 fusion.48
  39.3 50.1 %psum.42 = bf16[6,16,128]{2,1,0:T(8,128)(2,1)S(1)} all-reduce(f32[6,16,128]{2,1,0:T(8,128)S(1)} %fusion.23), channel_id=1, replica_groups=mesh['dp'=16,'tensor'=16] {'tensor'}, use_global_device_ids=true, to_apply=%region_0.0 | all-reduce | flops 12288 | bytes 73728 | tf_op jit(solution)/shard_map/psum | solution.py:60
  89.4 2.1 fusion.29
  91.6 167.9 %all-to-all-done = bf16[16,896,512]{2,1,0:T(8,128)(2,1)} async-done(((bf16[16,896,512]{2,1,0:T(8,128)(2,1)}), bf16[16,896,512]{2,1,0:T(8,128)(2,1)}, u32[]{:S(2)}, u32[]{:S(2)}) %all-to-all-start) | async-done | bytes 14680096 | tf_op jit(solution)/shard_map/all_to_all | solution.py:69
  259.5 16.5 %copy.56 = bf16[896,16,512]{2,1,0:T(8,128)(2,1)} copy(bf16[896,16,512]{2,0,1:T(8,128)(2,1)} %bitcast.2) | data formatting | bytes 29360128 | tf_op jit(solution)/shard_map/reshape | solution.py:68
  276.0 22.5 %reshape.345 = bf16[896,8192,1]{1,0,2:T(8,128)(2,1)} reshape(bf16[896,16,512]{2,1,0:T(8,128)(2,1)} %copy.56) | data formatting | bytes 29360128 | tf_op jit(solution)/shard_map/reshape | solution.py:68
  298.5 24.1 %fusion.10 = (bf16[6,128,896]{2,1,0:T(8,128)(2,1)}, bf16[6,128,896]{2,1,0:T(8,128)(2,1)}, bf16[6,128,896]{2,1,0:T(8,128)(2,1)S(1)}) fusion(bf16[6,128,896]{2,1,0:T(8,128)(2,1)} %bitcast.58, bf16[6,128,896]{2,1,0:T(8,128)(2,1)} %bitcast.59, f32[6,128,896]{2,1,0:T(8,128)} %fusion.29, bf16[6,128,8192]{2,1,0:T(8,128)(2,1)} %bitcast.57, ...), kind=kOutput, calls=%fused_computation.24 | convolution fusion | flops 11288051712 | bytes 36896768 | tf_op jit(solution)/shard_map/dot_general | solution.py:66
  322.7 2.6 convolution_multiply_fusion.4
  325.3 1.2 convolution_multiply_fusion.5
  327.3 47.8 %all-reduce.2 = (bf16[6,16,128]{2,1,0:T(8,128)(2,1)S(1)}, bf16[6,16,128]{2,1,0:T(8,128)(2,1)S(1)}, bf16[6,16,128]{2,1,0:T(8,128)(2,1)S(1)}, bf16[6,16,128]{2,1,0:T(8,128)(2,1)S(1)}, bf16[6,16,128]{2,1,0:T(8,128)(2,1)S(1)}) all-reduce(f32[6,16,128]{2,1,0:T(8,128)S(1)} %copy-done.15, ...), channel_id=1, replica_groups=mesh['dp'=16,'tensor'=16] {'tensor'}, use_global_device_ids=true, to_apply=%region_1.4 | all-reduce | flops 61440 | bytes 368640 | tf_op jit(solution)/shard_map/psum | solution.py:84
  375.4 1.8 fusion.17
  378.4 2.6 fusion
  381.0 1.7 copy.62
  382.8 29.3 %all-to-all-start.1 = ((bf16[16,1,16,4224]{3,2,1,0:T(8,128)(2,1)}), bf16[16,1,16,4224]{3,2,1,0:T(8,128)(2,1)S(1)}, u32[]{:S(2)}, u32[]{:S(2)}) async-start(bf16[16,1,16,4224]{3,2,1,0:T(8,128)(2,1)} %copy.62), calls=%async_computation.1 | async-start | bytes 4325376 | tf_op jit(solution)/shard_map/all_to_all | solution.py:138
  413.0 1.3 add_convert_fusion
  414.3 29.1 %all-to-all-done.1 = bf16[16,1,16,4224]{3,2,1,0:T(8,128)(2,1)S(1)} async-done(((bf16[16,1,16,4224]{3,2,1,0:T(8,128)(2,1)}), bf16[16,1,16,4224]{3,2,1,0:T(8,128)(2,1)S(1)}, u32[]{:S(2)}, u32[]{:S(2)}) %all-to-all-start.1) | async-done | bytes 2162720 | tf_op jit(solution)/shard_map/all_to_all | solution.py:138
  443.4 1.1 fusion.11
  444.8 0.7 copy.65
  445.4 0.7 copy.67
  446.1 0.7 copy.68
  (80 shorter events, 7.7 us)
Async XLA Ops:
  7.2 17.9 %copy-start = (bf16[48,16,896]{2,1,0:T(8,128)(2,1)S(1)}, bf16[48,16,896]{2,1,0:T(8,128)(2,1)}, u32[]{:S(2)}) copy-start(bf16[48,16,896]{2,1,0:T(8,128)(2,1)} %param.26) | copy-start | bytes 4128772
  7.2 291.4 %all-gather.2.cloned.1.call-start = ((), (), s32[]{:S(2)}) async-start(), calls=%async_computation.2 | async-start | bytes 13369344 | tf_op jit(solution)/shard_map/all_gather | solution.py:65
  15.7 7.4 %copy-start.22 = (s32[96]{0:T(128)S(1)}, s32[96]{0:T(128)}, u32[]{:S(2)}) copy-start(s32[96]{0:T(128)} %param.28) | copy-start | bytes 1156
  15.7 16.3 %copy-start.2 = (bf16[768,512]{1,0:T(8,128)(2,1)S(1)}, bf16[768,512]{1,0:T(8,128)(2,1)}, u32[]{:S(2)}) copy-start(bf16[768,512]{1,0:T(8,128)(2,1)} %param.18) | copy-start | bytes 2359300
  15.7 243.8 %all-to-all-start = ((bf16[16,896,512]{2,1,0:T(8,128)(2,1)}), bf16[16,896,512]{2,1,0:T(8,128)(2,1)}, u32[]{:S(2)}, u32[]{:S(2)}) async-start(bf16[16,896,512]{2,1,0:T(8,128)(2,1)} %stack.2), calls=%async_computation | async-start | bytes 29360128 | tf_op jit(solution)/shard_map/all_to_all | solution.py:69
  25.1 10.7 %copy-start.23 = (s32[48]{0:T(128)S(1)}, s32[48]{0:T(128)}, u32[]{:S(2)}) copy-start(s32[48]{0:T(128)} %param.29) | copy-start | bytes 580
  25.7 63.8 %copy-start.6 = (bf16[6,16,896]{2,1,0:T(8,128)(2,1)}, bf16[6,16,896]{2,1,0:T(8,128)(2,1)S(1)}, u32[]{:S(2)}) copy-start(bf16[6,16,896]{2,1,0:T(8,128)(2,1)S(1)} %gather_fusion.3) | copy-start | bytes 516100
  31.3 0.6 copy-start.10
  34.7 1.1 copy-start.8
  35.9 3.0 copy-start.3
  322.7 2.7 copy-start.5
  322.7 3.9 copy-start.7
  325.3 1.8 copy-start.12
  325.3 1.8 copy-start.13
  325.3 1.8 copy-start.14
  326.5 0.8 copy-start.15
  375.2 2.2 copy-start.16
  375.2 2.2 copy-start.18
  375.4 2.0 copy-start.4
  377.7 0.6 copy-start.20
  377.7 0.7 copy-start.21
  382.8 29.4 %copy-start.11 = (bf16[6,16,512]{2,1,0:T(8,128)(2,1)S(1)}, bf16[6,16,512]{2,1,0:T(8,128)(2,1)}, u32[]{:S(2)}) copy-start(bf16[6,16,512]{2,1,0:T(8,128)(2,1)} %copy-done.10) | copy-start | bytes 294916
  382.8 29.4 %copy-start.19 = (bf16[6,16,128]{2,1,0:T(8,128)(2,1)S(1)}, bf16[6,16,128]{2,1,0:T(8,128)(2,1)}, u32[]{:S(2)}) copy-start(bf16[6,16,128]{2,1,0:T(8,128)(2,1)} %copy-done.18) | copy-start | bytes 73732
  382.8 60.7 %all-to-all-start.1 = ((bf16[16,1,16,4224]{3,2,1,0:T(8,128)(2,1)}), bf16[16,1,16,4224]{3,2,1,0:T(8,128)(2,1)S(1)}, u32[]{:S(2)}, u32[]{:S(2)}) async-start(bf16[16,1,16,4224]{3,2,1,0:T(8,128)(2,1)} %copy.62), calls=%async_computation.1 | async-start | bytes 4325376 | tf_op jit(solution)/shard_map/all_to_all | solution.py:138
  412.1 0.9 copy-start.9
  412.1 0.9 copy-start.17
  444.5 4.3 copy-start.1
Sparse Core Ops, SparseCore 0:
  9.8 77.1 all-gather.1
